TPU v7x, 32 devices: a whole 2x2x4 slice. The times are simulated.
32 devices in a mesh: op: 4 (over z), row: 8 (over y, x, core).
Axes of the slice: x: 2, y: 2, z: 4, core: 2. Of those that a mesh axis runs over, the one named last changes fastest.
Arguments:
- wannier_ops: bfloat16 [2, 1000, 2, 128, 128], P(None, 'row'), may hold values from -0.1875 to 0.1875
- r_coords: int32 [1000, 3], P('row'), may hold values from -8 to 8
- degeneracy: int32 [1000], P('row'), may hold values from 1 to 4
- kpoints: int32 [64, 3], replicated, may hold values from 0 to 15
- bloch_vectors: bfloat16 [64, 2, 64, 128], P(('op', 'row')), may hold values from -0.375 to 0.375
Outputs:
- covariant: float32 [64, 2, 4096], P(('op', 'row'))
Inputs may be any that keep to these rules, and one draw needn't show every extreme that they name: `r_coords`: these coordinates are small integers; a program may pack several of them into one int32 word when it moves them. `degeneracy`: these degeneracies are small integers; a program may pack several of them into one int32 word when it moves them.
All inputs are finite; a program needn't handle non-finite values.
Results may differ from a plain program's by a relative error of at most 0.0038.
Values may be sent and summed in bfloat16 or wider, within the bound.
A program may use at most 192 MiB of HBM per device.

v0:
```python
import math

import jax
import jax.numpy as jnp
from jax import lax
from jax.sharding import PartitionSpec as P

GRID = 16
RMAX = 8


TWO_PI = 6.283185307179586
HIGH = lax.Precision.HIGHEST


def phase_parts(r_coords, degeneracy, kpoints):
    turns_int = jnp.sum(r_coords[:, None, :] * kpoints[None, :, :], axis=2) % GRID
    angles = turns_int.astype(jnp.float32) * (TWO_PI / GRID)
    weights = 1.0 / degeneracy.astype(jnp.float32)
    cosine = jnp.cos(angles) * weights[:, None]
    sine_part = jnp.sin(angles) * weights[:, None]
    along_x = (r_coords[:, 0].astype(jnp.float32) / RMAX)[:, None]
    return (cosine, sine_part, along_x)


def fourier(phase_re, phase_im, flat_ops):
    stacked = jnp.concatenate([phase_re, phase_im], axis=1)
    product_sum = lax.dot_general(
        stacked, flat_ops, (((0,), (0,)), ((), ())), preferred_element_type=jnp.float32
    )
    k_count = phase_re.shape[1]
    half_cols = flat_ops.shape[1] // 2
    real_part = product_sum[:k_count, :half_cols] - product_sum[k_count:, half_cols:]
    imag_part = product_sum[:k_count, half_cols:] + product_sum[k_count:, :half_cols]
    return (real_part, imag_part)


def complex_mul(form, left, right):

    def single(first, second):
        return jnp.einsum(form, first, second, precision=HIGH)

    return (
        single(left[0], right[0]) - single(left[1], right[1]),
        single(left[0], right[1]) + single(left[1], right[0]),
    )


def rotate(op_pair, vec_pair):
    left_side = complex_mul("knm,kmp->knp", (vec_pair[0], -vec_pair[1]), op_pair)
    return complex_mul("knm,kpm->knp", left_side, vec_pair)


def covariant_form(ham, deriv, posit, posit_deriv):
    band_count = ham[0].shape[-1]
    factor = 1.0 / math.sqrt(band_count)
    form = "kab,kbc->kac"
    a_d = complex_mul(form, posit, deriv)
    d_a = complex_mul(form, deriv, posit)
    h_a = complex_mul(form, ham, posit)
    a_h = complex_mul(form, posit, ham)
    g_real = posit_deriv[0] + factor * (h_a[0] + a_h[0] - (a_d[1] - d_a[1]))
    g_imag = posit_deriv[1] + factor * (h_a[1] + a_h[1] + (a_d[0] - d_a[0]))
    k_count = g_real.shape[0]
    return jnp.stack([g_real.reshape(k_count, -1), g_imag.reshape(k_count, -1)], axis=1)


def make_phases(coords, degens, kpoints, derive):
    cosine, sine_part, along_x = phase_parts(coords, degens, kpoints)
    phase_re = jnp.where(derive, -along_x * sine_part, cosine).astype(jnp.bfloat16)
    phase_im = jnp.where(derive, along_x * cosine, sine_part).astype(jnp.bfloat16)
    return (phase_re, phase_im)


def on_device(wannier_ops, r_coords, degeneracy, kpoints, bloch_vectors):
    row_count = lax.axis_size("row")
    op_count = lax.axis_size("op")
    component = lax.axis_index("op")
    base_ops = lax.dynamic_index_in_dim(wannier_ops, component // 2, 0, keepdims=False)
    r_local = base_ops.shape[0]
    width = base_ops.shape[-1]
    derive = component % 2 == 1
    total_k = kpoints.shape[0]
    per_block = total_k // (row_count * op_count)
    owned_rows = total_k // row_count
    vectors = bloch_vectors.astype(jnp.float32)
    vec_pair = (vectors[:, 0], vectors[:, 1])
    flat_ops = base_ops.reshape(r_local, 2 * width * width)
    phase_re, phase_im = make_phases(r_coords, degeneracy, kpoints, derive)
    rows_here = lax.iota(jnp.int32, owned_rows * lax.axis_size("row"))
    owner = rows_here // (op_count * per_block)
    group = rows_here // per_block % op_count
    offset = rows_here % per_block
    picked = group * (row_count * per_block) + owner * per_block + offset
    pair, picked = (
        fourier(jnp.take(phase_re, picked, axis=1), jnp.take(phase_im, picked, axis=1), flat_ops),
        picked,
    )
    summed = lax.psum_scatter(
        jnp.stack([pair[0], pair[1]], axis=1), "row", scatter_dimension=0, tiled=True
    )
    last_cols = summed.shape[-1]
    blocks = summed.reshape(op_count, 1, per_block, 2, last_cols)
    regrouped = lax.all_to_all(blocks, "op", split_axis=0, concat_axis=1, tiled=True)
    pieces = regrouped.reshape(op_count, per_block, 2, last_cols)
    rotated = []
    for component_id in range(4):
        op_pair = (
            pieces[component_id, :, 0].reshape(per_block, width, width),
            pieces[component_id, :, 1].reshape(per_block, width, width),
        )
        rotated.append(rotate(op_pair, vec_pair))
    return covariant_form(rotated[0], rotated[1], rotated[2], rotated[3])


def solution(mesh):
    in_specs = (
        P(None, "row", None, None, None),
        P("row", None),
        P("row"),
        P(),
        P(("op", "row"), None, None, None),
    )
    out_specs = P(("op", "row"), None, None)
    return jax.shard_map(
        on_device, mesh=mesh, in_specs=in_specs, out_specs=out_specs, check_vma=False
    )
```

profile of v0, /device:TPU:0, one launch (start us, length us, event | category | flops | bytes accessed | tf_op | source)
XLA Modules:
  0.0 183.5 jit_solution(6121293962703633077)
XLA Ops:
  6.6 0.7 convert_divide_fusion
  7.2 0.7 negate_bitcast_fusion
  7.9 0.8 multiply_reduce_fusion
  8.9 0.6 gather_fusion
  9.5 0.6 gather_fusion.1
  10.2 10.1 %constant_dynamic-slice_fusion = bf16[1,125,2,128,128]{4,3,2,1,0:T(8,128)(2,1)} fusion(bf16[2,125,2,128,128]{4,3,2,1,0:T(8,128)(2,1)} %param.7, s32[]{:T(128)S(6)} %select_n.75), kind=kLoop, calls=%fused_computation.178 | loop fusion | bytes 16384004 | tf_op jit(solution)/shard_map/jit(dynamic_index_in_dim)/dynamic_slice | solution.py:79
  20.3 13.3 %reshape.24 = bf16[125,32768]{1,0:T(8,128)(2,1)} reshape(bf16[1,125,2,128,128]{4,3,2,1,0:T(8,128)(2,1)} %constant_dynamic-slice_fusion) | data formatting | bytes 16384000 | tf_op jit(solution)/shard_map/reshape | solution.py:88
  33.6 11.4 %fusion.63 = f32[128,32768]{1,0:T(8,128)} fusion(bf16[125,32768]{1,0:T(8,128)(2,1)} %reshape.24, bf16[125,64]{0,1:T(8,128)(2,1)S(1)} %get-tuple-element.21, bf16[125,64]{0,1:T(8,128)(2,1)S(1)} %get-tuple-element.20), kind=kOutput, calls=%fused_computation.106 | convolution fusion | flops 1048640000 | bytes 25001216 | tf_op jit(solution)/shard_map/dot_general | solution.py:28
  45.1 8.6 %fusion.1 = (f32[64,1,16384]{2,0,1:T(8,128)S(1)}, f32[64,1,16384]{2,0,1:T(8,128)}) fusion(f32[128,32768]{1,0:T(8,128)} %fusion.63), kind=kLoop, calls=%fused_computation.6 | loop fusion | flops 2097152 | bytes 25165824 | tf_op jit(solution)/shard_map/stack | solution.py:100
  53.7 6.0 %pad_maximum_fusion = f32[64,2,16384]{2,0,1:T(8,128)} fusion(f32[64,1,16384]{2,0,1:T(8,128)} %get-tuple-element.7, f32[64,1,16384]{2,0,1:T(8,128)S(1)} %get-tuple-element.6), kind=kLoop, calls=%fused_computation.2 | loop fusion | flops 2097152 | bytes 16777216 | tf_op jit(solution)/shard_map/stack | solution.py:100
  59.8 74.3 %reduce-scatter.2.cloned.1.call-done = f32[8,2,16384]{2,0,1:T(8,128)} async-done(((f32[64,2,16384]{2,0,1:T(8,128)}), f32[8,2,16384]{2,0,1:T(8,128)}) %reduce-scatter.2.cloned.1.call-update) | async-done | bytes 1048592 | tf_op jit(solution)/shard_map/reduce_scatter | solution.py:99
  134.1 1.8 %reshape.25 = f32[4,1,2,2,16384]{4,2,0,3,1:T(2,128)S(1)} reshape(f32[8,2,16384]{2,0,1:T(8,128)} %reduce-scatter.2.cloned.1.call-done) | data formatting | bytes 2097152 | tf_op jit(solution)/shard_map/reshape | solution.py:103
  136.0 29.9 %all_to_all.4 = f32[4,1,2,2,16384]{4,2,3,1,0:T(2,128)S(1)} all-to-all(f32[4,1,2,2,16384]{4,2,3,1,0:T(2,128)S(1)} %copy.19), channel_id=1, replica_groups=mesh['op'=4,'row'=8] {'op'}, dimensions={0} | all-to-all | bytes 2097152 | tf_op jit(solution)/shard_map/all_to_all | solution.py:104
  166.0 0.2 fusion.30
  166.2 0.2 fusion.34
  166.4 0.2 convolution_subtract_fusion.11
  167.0 0.2 fusion.12
  167.2 0.2 fusion.16
  167.4 0.2 convolution_subtract_fusion.3
  168.1 0.2 fusion.18
  168.2 0.2 fusion.22
  168.4 0.2 convolution_subtract_fusion.7
  169.1 0.2 convolution_add_fusion.6
  169.3 0.2 convolution_add_fusion.9
  169.9 0.2 fusion.153
  170.1 0.2 fusion.152
  170.3 0.2 fusion.24
  170.5 0.2 fusion.28
  170.7 0.2 convolution_subtract_fusion.9
  171.3 0.2 convolution_add_fusion.7
  171.5 0.2 fusion.149
  171.7 0.2 convolution_add_fusion.10
  172.2 0.2 fusion.150
  172.4 0.2 fusion.147
  172.6 0.2 fusion.146
  172.8 0.2 convolution_add_fusion.11
  173.2 0.2 fusion.148
  173.4 0.2 convolution_subtract_fusion.1
  173.6 0.2 convolution_add_fusion.4
  174.0 0.2 fusion.151
  174.2 0.2 convolution_add_fusion.1
  174.4 0.2 convolution_subtract_fusion.5
  174.6 0.2 fusion.8
  174.8 0.2 fusion.10
  175.3 0.2 fusion.4
  175.5 0.2 fusion.11
  175.7 0.2 fusion.5
  176.0 0.7 pad_maximum_fusion.1
  (27 shorter events, 3.1 us)
Async XLA Ops:
  6.5 127.6 %reduce-scatter.2.cloned.1.call-start = ((), (), s32[]{:S(2)}) async-start(), calls=%async_computation.2 | async-start | bytes 9437184 | tf_op jit(solution)/shard_map/reduce_scatter | solution.py:99
  59.8 106.2 %copy-start = (bf16[2,2,64,128]{3,2,1,0:T(8,128)(2,1)S(1)}, bf16[2,2,64,128]{3,2,1,0:T(8,128)(2,1)}, u32[]{:S(2)}) copy-start(bf16[2,2,64,128]{3,2,1,0:T(8,128)(2,1)} %param.11) | copy-start | bytes 196612
Sparse Core Ops, SparseCore 0:
  59.9 74.1 reduce-scatter.1
where the time goes:
time: 184 us
  waiting for transfers between devices  74.3 us (40%)
  blocking collectives  29.9 us (16%)
  local copies, waits for them, and re-layouts  26.9 us (15%)
  matrix products  20.8 us (11%)
  other arithmetic  17.8 us (10%)
  between operations  13.8 us (8%)
    reduce_scatter x1, waiting for transfers between devices, on_device(): lax.psum_scatter(jnp.stack([pair[0], pair[1]], axis=1), 'row', scatter_di...  74.3 us
    all_to_all x1, blocking collectives, on_device(): lax.all_to_all(blocks, 'op', split_axis=0, concat_axis=1, tiled=True)  29.9 us
    another operation x2, other arithmetic, on_device(): jnp.stack([pair[0], pair[1]], axis=1)  14.7 us
    reshape x1, local copies, waits for them, and re-layouts, on_device(): flat_ops = base_ops.reshape(r_local, 2 * width * width)  13.3 us
    dot_general x1, matrix products, fourier(): lax.dot_general(stacked, flat_ops, (((0,), (0,)), ((), ())), preferred_el...  11.4 us
    dynamic_slice x1, local copies, waits for them, and re-layouts, on_device(): lax.dynamic_index_in_dim(wannier_ops, component // 2, 0, keepdims=False)  10.1 us
    dot_general x48, matrix products, single(): return jnp.einsum(form, first, second, precision=HIGH)  9.35 us
  transfers between devices with their start and end apart: 1, of which 1 were waited for; matrix products, arithmetic and copies ran while one was open for 0% of the time, Pallas kernels for 0%

commit v1 on v0

v1 whole, which is shorter than its diff:
```python
import functools
import math

import jax
import jax.numpy as jnp
from jax import lax
from jax.experimental import pallas as pl
from jax.experimental.pallas import tpu as pltpu
from jax.sharding import PartitionSpec as P

GRID = 16
RMAX = 8
TWO_PI = 6.283185307179586
STEP = 16
AHEAD = 6
PITCH_PAD = 8
MESH = pl.DeviceIdType.MESH
F32 = jnp.float32
BF16 = jnp.bfloat16
NT = (((1,), (1,)), ((), ()))
NN = (((1,), (0,)), ((), ()))


def mm(a, b, dims=NN, precision=None):
    return lax.dot_general(a, b, dims, preferred_element_type=F32, precision=precision)


def kernel(
    n, ops_ref, rc_ref, deg_ref, kp_ref, v_ref, out_ref,
    obuf, cast, phase, rcs, degs, fsum, vall, sbuf, rbuf, own,
    osem, lsem, vsend, vrecv, bsend, brecv,
):
    me = lax.axis_index("row")
    group = lax.axis_index("op")
    r_local, width = ops_ref.shape[1], ops_ref.shape[-1]
    r_pad = cast.shape[0]
    pitch = cast.shape[1]
    bands = v_ref.shape[2]
    per = v_ref.shape[0]
    k_group = n * per
    rows = 4 * k_group
    fpitch = fsum.shape[1]
    blocks = width // STEP
    total = 2 * blocks

    def op_copy(t):
        return pltpu.make_async_copy(
            ops_ref.at[t // blocks, :, :, pl.ds((t % blocks) * STEP, STEP), :],
            obuf.at[t],
            osem.at[t],
        )

    for t in range(min(AHEAD, total)):
        op_copy(t).start()

    barrier = pltpu.get_barrier_semaphore()

    def greet(s, carry):
        pl.semaphore_signal(barrier, inc=1, device_id={"row": lax.rem(me + s, n)}, device_id_type=MESH)
        return carry

    lax.fori_loop(1, n, greet, 0)

    local_v = pltpu.make_async_copy(v_ref, vall.at[me], lsem)
    local_v.start()

    rcs[...] = jnp.zeros_like(rcs)
    rcs[pl.ds(0, r_local), :] = rc_ref[...].astype(F32)
    degs[...] = jnp.ones_like(degs)
    degs[:, pl.ds(0, r_local)] = deg_ref[...].astype(F32)
    coords = rcs[...].astype(BF16)
    points = kp_ref[pl.ds(pl.multiple_of(group * k_group, k_group), k_group), :].astype(F32).astype(BF16)
    inner = mm(points, coords, NT)
    pick = (lax.broadcasted_iota(jnp.int32, points.shape, 1) == 0).astype(F32).astype(BF16)
    along_x = mm(pick, coords, NT) / RMAX
    turns = inner - GRID * jnp.floor(inner / GRID)
    angles = turns * (TWO_PI / GRID)
    live = lax.broadcasted_iota(jnp.int32, inner.shape, 1) < r_local
    weights = jnp.where(live, 1.0 / degs[...], 0.0)
    cosine = jnp.cos(angles) * weights
    sine = jnp.sin(angles) * weights
    for comp, (re, im) in enumerate(((cosine, sine), (-along_x * sine, along_x * cosine))):
        base = comp * 2 * k_group
        phase[pl.ds(base, k_group), :] = jnp.concatenate([re, -im], axis=1).astype(BF16)
        phase[pl.ds(base + k_group, k_group), :] = jnp.concatenate([im, re], axis=1).astype(BF16)
    if r_pad > r_local:
        cast[pl.ds(r_local, r_pad - r_local)] = jnp.zeros((r_pad - r_local, pitch, width), F32)

    pl.semaphore_wait(barrier, n - 1)

    def v_copy(s):
        to = lax.rem(me + s, n)
        return pltpu.make_async_remote_copy(
            src_ref=v_ref, dst_ref=vall.at[me], send_sem=vsend.at[to], recv_sem=vrecv.at[me],
            device_id={"row": to}, device_id_type=MESH,
        )

    def v_start(s, carry):
        v_copy(s).start()
        return carry

    lax.fori_loop(1, n, v_start, 0)

    cast_rows = cast.reshape(r_pad * pitch, width)
    fsum_rows = fsum.reshape(width * fpitch, width)

    def fourier(op):
        def body(i, carry):
            t = op * blocks + i
            op_copy(t).wait()

            @pl.when(t + AHEAD < total)
            def _():
                op_copy(t + AHEAD).start()

            cast[pl.ds(0, r_local), pl.ds(0, 2 * STEP), :] = (
                obuf[t].astype(F32).reshape(r_local, 2 * STEP, width)
            )
            left = phase[...]
            for q in range(0, STEP, 2):
                sides = []
                for m in (q, q + 1):
                    parts = [
                        cast_rows[pl.ds(p * STEP + m, r_pad, stride=pitch), :].astype(BF16)
                        for p in range(2)
                    ]
                    sides.append(jnp.concatenate(parts, axis=0))
                got = mm(left, jnp.concatenate(sides, axis=1))
                fsum[i * STEP + q, pl.ds(0, rows), :] = got[:, :width]
                fsum[i * STEP + q + 1, pl.ds(0, rows), :] = got[:, width:]
            return carry

        lax.fori_loop(0, blocks, body, 0)

    def band_blocks(owner, kk):
        v_re, v_im = vall[owner, kk, 0], vall[owner, kk, 1]
        first = jnp.concatenate([v_re, -v_im], axis=1)
        second = jnp.concatenate([v_im, v_re], axis=1)
        third = jnp.concatenate([-v_re, v_im], axis=1)
        right = jnp.concatenate([first, second, second, third], axis=0)
        lefts = []
        for comp in range(2):
            row = comp * 2 * k_group + owner * per + kk
            re = fsum_rows[pl.ds(row, width, stride=fpitch), :].astype(BF16)
            im = fsum_rows[pl.ds(row + k_group, width, stride=fpitch), :].astype(BF16)
            lefts.append(jnp.concatenate([re, im], axis=1))
        g = mm(jnp.concatenate(lefts, axis=0), right, NT).astype(BF16)
        cols = 2 * bands
        stacks = [
            jnp.concatenate(
                [g[c * width:(c + 1) * width, :cols], g[c * width:(c + 1) * width, cols:]], axis=0
            )
            for c in range(2)
        ]
        b = mm(jnp.concatenate([v_re, v_im], axis=1), jnp.concatenate(stacks, axis=1))
        return b[:, :cols], b[:, cols:]

    def b_copy(op, to):
        return pltpu.make_async_remote_copy(
            src_ref=sbuf.at[op, to], dst_ref=rbuf.at[op, me],
            send_sem=bsend.at[op, to], recv_sem=brecv.at[op, me],
            device_id={"row": to}, device_id_type=MESH,
        )

    def v_wait(src):
        pltpu.make_async_remote_copy(
            src_ref=v_ref, dst_ref=vall.at[src], send_sem=vsend.at[src], recv_sem=vrecv.at[src],
            device_id={"row": src}, device_id_type=MESH,
        ).wait()

    def b_wait(op, src):
        pltpu.make_async_remote_copy(
            src_ref=sbuf.at[op, src], dst_ref=rbuf.at[op, src],
            send_sem=bsend.at[op, src], recv_sem=brecv.at[op, src],
            device_id={"row": src}, device_id_type=MESH,
        ).wait()

    for op in range(2):
        fourier(op)

        def send(s, carry):
            to = lax.rem(me + s, n)
            if op == 0:
                v_wait(to)
            for kk in range(per):
                for comp, b in enumerate(band_blocks(to, kk)):
                    sbuf[op, to, kk, comp] = b.astype(BF16)
            b_copy(op, to).start()
            return carry

        lax.fori_loop(1, n, send, 0)
        if op == 0:
            local_v.wait()
        for kk in range(per):
            for comp, b in enumerate(band_blocks(me, kk)):
                own[op, kk, comp] = b

    for op in range(2):

        def take(s, carry):
            src = lax.rem(me + s, n)
            b_wait(op, src)
            own[op] = own[op] + rbuf[op, src].astype(F32)
            return carry

        lax.fori_loop(1, n, take, 0)

    factor = 1.0 / math.sqrt(bands)

    def turn(m):
        return jnp.concatenate([-m[:, bands:], m[:, :bands]], axis=1)

    for kk in range(per):
        ham, deriv, posit, last = own[0, kk, 0], own[0, kk, 1], own[1, kk, 0], own[1, kk, 1]
        i_deriv = turn(deriv)
        plus, minus = ham + i_deriv, ham - i_deriv
        left = jnp.concatenate([posit, minus], axis=1)
        right = jnp.concatenate([plus, turn(plus), posit, turn(posit)], axis=0)
        res = last + factor * mm(left, right, NN, lax.Precision.HIGHEST)
        out_ref[kk, 0] = res[:, :bands]
        out_ref[kk, 1] = res[:, bands:]


def on_device(wannier_ops, r_coords, degeneracy, kpoints, bloch_vectors):
    n = lax.axis_size("row")
    r_local, width = wannier_ops.shape[1], wannier_ops.shape[-1]
    per, _, bands, _ = bloch_vectors.shape
    r_pad = -(-r_local // 128) * 128
    k_group = n * per
    total = 2 * (width // STEP)
    vmem = pl.BlockSpec(memory_space=pltpu.VMEM)
    dma = pltpu.SemaphoreType.DMA
    res = pl.pallas_call(
        functools.partial(kernel, n),
        out_shape=jax.ShapeDtypeStruct((per, 2, bands, bands), F32),
        in_specs=[pl.BlockSpec(memory_space=pl.ANY), vmem, vmem, vmem, vmem],
        out_specs=vmem,
        scratch_shapes=[
            pltpu.VMEM((total, r_local, 2, STEP, width), BF16),
            pltpu.VMEM((r_pad, 2 * STEP + PITCH_PAD, width), F32),
            pltpu.VMEM((4 * k_group, 2 * r_pad), BF16),
            pltpu.VMEM((r_pad, 3), F32),
            pltpu.VMEM((1, r_pad), F32),
            pltpu.VMEM((width, 4 * k_group + PITCH_PAD, width), F32),
            pltpu.VMEM((n, per, 2, bands, width), BF16),
            pltpu.VMEM((2, n, per, 2, bands, 2 * bands), BF16),
            pltpu.VMEM((2, n, per, 2, bands, 2 * bands), BF16),
            pltpu.VMEM((2, per, 2, bands, 2 * bands), F32),
            dma((total,)),
            dma,
            dma((n,)),
            dma((n,)),
            dma((2, n)),
            dma((2, n)),
        ],
        compiler_params=pltpu.CompilerParams(
            collective_id=0, has_side_effects=True, vmem_limit_bytes=62 * 1024 * 1024
        ),
    )(wannier_ops, r_coords, degeneracy.reshape(1, r_local), kpoints, bloch_vectors)
    return res.reshape(per, 2, bands * bands)


def solution(mesh):
    in_specs = (
        P(None, "row", None, None, None),
        P("row", None),
        P("row"),
        P(),
        P(("op", "row"), None, None, None),
    )
    out_specs = P(("op", "row"), None, None)
    return jax.shard_map(
        on_device, mesh=mesh, in_specs=in_specs, out_specs=out_specs, check_vma=False
    )
```

time: 184 us -> 37.1 us (0.20)
  the two profiles are of different devices: /device:TPU:0 before, /device:TPU:27 now
where the time goes in v1:
time: 37.1 us; the launch traced here: 36.8 us
  Pallas kernels  32.4 us (87%)
  local copies, waits for them, and re-layouts  4.43 us (12%)
    pallas_call x1, Pallas kernels, on_device(): pl.pallas_call(functools.partial(kernel, n), out_shape=jax.ShapeDtypeStru...  32.4 us
    unnamed x2, local copies, waits for them, and re-layouts  2.79 us
    reshape x1, local copies, waits for them, and re-layouts, on_device(): return res.reshape(per, 2, bands * bands)  1.64 us

profile of v1, /device:TPU:27, one launch (start us, length us, event | category | flops | bytes accessed | tf_op | source)
XLA Modules:
  0.0 36.8 jit_solution(5778299115946000101)
XLA Ops:
  0.0 1.4 %copy.7.kp_ref = s32[64,3]{1,0:T(8,128)} copy(s32[64,3]{0,1:T(4,128)} %param.8) | data formatting | bytes 1536 | tf_op args[3]
  1.4 1.4 %copy.6.rc_ref = s32[125,3]{1,0:T(8,128)} copy(s32[125,3]{0,1:T(4,128)} %param.6) | data formatting | bytes 3000 | tf_op args[1]
  2.8 32.4 %shard_map.55 = f32[2,2,64,64]{3,2,1,0:T(8,128)} custom-call(bf16[2,125,2,128,128]{4,3,2,1,0:T(8,128)(2,1)} %ops_ref.1, s32[125,3]{1,0:T(8,128)} %copy.6.rc_ref, s32[1,125]{1,0:T(1,128)} %bitcast.3, s32[64,3]{1,0:T(8,128)} %copy.7.kp_ref, bf16[2,2,64,128]{3,2,1,0:T(8,128)(2,1)} %v_ref.1), custom_call_target="tpu_custom_call" | custom-call | tf_op jit(solution)/shard_map/pallas_call | solution.py:233
  35.2 1.6 %reshape.7 = f32[2,2,4096]{2,1,0:T(2,128)} reshape(f32[2,2,64,64]{3,2,1,0:T(8,128)} %shard_map.55) | data formatting | bytes 131072 | tf_op jit(solution)/shard_map/reshape | solution.py:260

commit v2 on v1

--- a/solution.py
+++ b/solution.py
@@ -27,7 +27,7 @@
 
 def kernel(
     n, ops_ref, rc_ref, deg_ref, kp_ref, v_ref, out_ref,
-    obuf, cast, phase, rcs, degs, fsum, vall, sbuf, rbuf, own,
+    obuf, cast, phase, rcs, kps, inners, degs, fsum, vall, sbuf, rbuf, own,
     osem, lsem, vsend, vrecv, bsend, brecv,
 ):
     me = lax.axis_index("row")
@@ -65,14 +65,15 @@
     local_v.start()
 
     rcs[...] = jnp.zeros_like(rcs)
-    rcs[pl.ds(0, r_local), :] = rc_ref[...].astype(F32)
+    rcs[pl.ds(0, 3), pl.ds(0, r_local)] = rc_ref[...].astype(F32)
+    kps[...] = jnp.zeros_like(kps)
+    kps[pl.ds(0, 3), :] = kp_ref[...].astype(F32)
     degs[...] = jnp.ones_like(degs)
     degs[:, pl.ds(0, r_local)] = deg_ref[...].astype(F32)
     coords = rcs[...].astype(BF16)
-    points = kp_ref[pl.ds(pl.multiple_of(group * k_group, k_group), k_group), :].astype(F32).astype(BF16)
-    inner = mm(points, coords, NT)
-    pick = (lax.broadcasted_iota(jnp.int32, points.shape, 1) == 0).astype(F32).astype(BF16)
-    along_x = mm(pick, coords, NT) / RMAX
+    inners[...] = mm(kps[...].astype(BF16), coords, (((0,), (0,)), ((), ())))
+    inner = inners[pl.ds(pl.multiple_of(group * k_group, k_group), k_group), :]
+    along_x = rcs[pl.ds(0, 1), :] / RMAX
     turns = inner - GRID * jnp.floor(inner / GRID)
     angles = turns * (TWO_PI / GRID)
     live = lax.broadcasted_iota(jnp.int32, inner.shape, 1) < r_local
@@ -239,7 +240,9 @@
             pltpu.VMEM((total, r_local, 2, STEP, width), BF16),
             pltpu.VMEM((r_pad, 2 * STEP + PITCH_PAD, width), F32),
             pltpu.VMEM((4 * k_group, 2 * r_pad), BF16),
-            pltpu.VMEM((r_pad, 3), F32),
+            pltpu.VMEM((8, r_pad), F32),
+            pltpu.VMEM((8, kpoints.shape[0]), F32),
+            pltpu.VMEM((kpoints.shape[0], r_pad), F32),
             pltpu.VMEM((1, r_pad), F32),
             pltpu.VMEM((width, 4 * k_group + PITCH_PAD, width), F32),
             pltpu.VMEM((n, per, 2, bands, width), BF16),
@@ -256,7 +259,7 @@
         compiler_params=pltpu.CompilerParams(
             collective_id=0, has_side_effects=True, vmem_limit_bytes=62 * 1024 * 1024
         ),
-    )(wannier_ops, r_coords, degeneracy.reshape(1, r_local), kpoints, bloch_vectors)
+    )(wannier_ops, r_coords.T, degeneracy.reshape(1, r_local), kpoints.T, bloch_vectors)
     return res.reshape(per, 2, bands * bands)
 
 

time: 37.1 us -> 34.2 us (0.922)
  local copies, waits for them, and re-layouts: 4.43 us -> 1.64 us
    unnamed x2 -> x0, local copies, waits for them, and re-layouts: 2.79 us -> none
where the time goes in v2:
time: 34.2 us; the launch traced here: 34 us
  Pallas kernels  32.4 us (95%)
  local copies, waits for them, and re-layouts  1.64 us (5%)
    pallas_call x1, Pallas kernels, on_device(): pl.pallas_call(functools.partial(kernel, n), out_shape=jax.ShapeDtypeStru...  32.4 us
    reshape x1, local copies, waits for them, and re-layouts, on_device(): return res.reshape(per, 2, bands * bands)  1.64 us

profile of v2, /device:TPU:27, one launch (start us, length us, event | category | flops | bytes accessed | tf_op | source)
XLA Modules:
  0.0 34.0 jit_solution(2226674757779599817)
XLA Ops:
  0.0 32.4 %shard_map.55 = f32[2,2,64,64]{3,2,1,0:T(8,128)} custom-call(bf16[2,125,2,128,128]{4,3,2,1,0:T(8,128)(2,1)} %ops_ref.1, s32[3,125]{1,0:T(4,128)} %bitcast.5, s32[1,125]{1,0:T(1,128)} %bitcast.7, s32[3,64]{1,0:T(4,128)} %bitcast.6, bf16[2,2,64,128]{3,2,1,0:T(8,128)(2,1)} %v_ref.1), custom_call_target="tpu_custom_call" | custom-call | tf_op jit(solution)/shard_map/pallas_call | solution.py:234
  32.4 1.6 %reshape.7 = f32[2,2,4096]{2,1,0:T(2,128)} reshape(f32[2,2,64,64]{3,2,1,0:T(8,128)} %shard_map.55) | data formatting | bytes 131072 | tf_op jit(solution)/shard_map/reshape | solution.py:263

commit v3 on v2

--- a/solution.py
+++ b/solution.py
@@ -33,8 +33,8 @@
     me = lax.axis_index("row")
     group = lax.axis_index("op")
     r_local, width = ops_ref.shape[1], ops_ref.shape[-1]
-    r_pad = cast.shape[0]
-    pitch = cast.shape[1]
+    pitch = 2 * STEP + 1
+    r_pad = cast.shape[0] // pitch
     bands = v_ref.shape[2]
     per = v_ref.shape[0]
     k_group = n * per
@@ -85,7 +85,8 @@
         phase[pl.ds(base, k_group), :] = jnp.concatenate([re, -im], axis=1).astype(BF16)
         phase[pl.ds(base + k_group, k_group), :] = jnp.concatenate([im, re], axis=1).astype(BF16)
     if r_pad > r_local:
-        cast[pl.ds(r_local, r_pad - r_local)] = jnp.zeros((r_pad - r_local, pitch, width), F32)
+        tail = (r_pad - r_local) * pitch
+        cast[pl.ds(r_local * pitch, tail), :] = jnp.zeros((tail, width), F32)
 
     pl.semaphore_wait(barrier, n - 1)
 
@@ -102,7 +103,7 @@
 
     lax.fori_loop(1, n, v_start, 0)
 
-    cast_rows = cast.reshape(r_pad * pitch, width)
+    cast_rows = cast
     fsum_rows = fsum.reshape(width * fpitch, width)
 
     def fourier(op):
@@ -114,9 +115,10 @@
             def _():
                 op_copy(t + AHEAD).start()
 
-            cast[pl.ds(0, r_local), pl.ds(0, 2 * STEP), :] = (
-                obuf[t].astype(F32).reshape(r_local, 2 * STEP, width)
-            )
+            for r in range(r_local):
+                cast[pl.ds(r * pitch, 2 * STEP), :] = (
+                    obuf[t, r].astype(F32).reshape(2 * STEP, width)
+                )
             left = phase[...]
             for q in range(0, STEP, 2):
                 sides = []
@@ -238,7 +240,7 @@
         out_specs=vmem,
         scratch_shapes=[
             pltpu.VMEM((total, r_local, 2, STEP, width), BF16),
-            pltpu.VMEM((r_pad, 2 * STEP + PITCH_PAD, width), F32),
+            pltpu.VMEM((r_pad * (2 * STEP + 1), width), F32),
             pltpu.VMEM((4 * k_group, 2 * r_pad), BF16),
             pltpu.VMEM((8, r_pad), F32),
             pltpu.VMEM((8, kpoints.shape[0]), F32),

time: 34.2 us -> 33.3 us (0.974)
  Pallas kernels: 32.4 us -> 31.4 us
    pallas_call x1, Pallas kernels: 32.4 us -> 31.4 us  [on_device(): pl.pallas_call(functools.partial(kernel, n), out_shape=jax.ShapeDtypeStru...]
where the time goes in v3:
time: 33.3 us; the launch traced here: 33.1 us
  Pallas kernels  31.4 us (94%)
  local copies, waits for them, and re-layouts  1.64 us (5%)
    pallas_call x1, Pallas kernels, on_device(): pl.pallas_call(functools.partial(kernel, n), out_shape=jax.ShapeDtypeStru...  31.4 us
    reshape x1, local copies, waits for them, and re-layouts, on_device(): return res.reshape(per, 2, bands * bands)  1.64 us

profile of v3, /device:TPU:27, one launch (start us, length us, event | category | flops | bytes accessed | tf_op | source)
XLA Modules:
  0.0 33.1 jit_solution(814539611641439041)
XLA Ops:
  0.0 31.4 %shard_map.55 = f32[2,2,64,64]{3,2,1,0:T(8,128)} custom-call(bf16[2,125,2,128,128]{4,3,2,1,0:T(8,128)(2,1)} %ops_ref.1, s32[3,125]{1,0:T(4,128)} %bitcast.5, s32[1,125]{1,0:T(1,128)} %bitcast.7, s32[3,64]{1,0:T(4,128)} %bitcast.6, bf16[2,2,64,128]{3,2,1,0:T(8,128)(2,1)} %v_ref.1), custom_call_target="tpu_custom_call" | custom-call | tf_op jit(solution)/shard_map/pallas_call | solution.py:236
  31.5 1.6 %reshape.7 = f32[2,2,4096]{2,1,0:T(2,128)} reshape(f32[2,2,64,64]{3,2,1,0:T(8,128)} %shard_map.55) | data formatting | bytes 131072 | tf_op jit(solution)/shard_map/reshape | solution.py:265
